TPU v7x, 512 devices: a whole 4x4x16 slice. The times are simulated.
512 devices in a mesh: grp: 8 (over y, x_hi), comp: 64 (over x_lo, z, core).
Axes of the slice: x: 4 (x_hi: 2, x_lo: 2; x = x_hi * 2 + x_lo), y: 4, z: 16, core: 2. Of those that a mesh axis runs over, the one named last changes fastest.
Arguments:
- features: bfloat16 [1048576, 256], P(('grp', 'comp')), may hold values from -8 to 8
- means: float32 [1024, 256], P('comp'), may hold values from -1 to 1
- variances: float32 [1024, 256], P('comp'), may hold values from 0.5 to 2
- weight_logits: float32 [1024], replicated, may hold values from -1 to 1
Outputs:
- new_means: float32 [1024, 256], replicated
- new_variances: float32 [1024, 256], replicated
- new_log_weights: float32 [1024], replicated
- row_scores: float32 [1048576], P(('grp', 'comp'))
All inputs are finite; a program needn't handle non-finite values.
Results may differ from a plain program's by a relative error of at most 0.00085.
Values sent between devices are 32-bit elements; how exact they have to be, the bound alone decides.
A program may use at most 64 MiB of HBM per device.

v0:
```python
import math

import jax
import jax.numpy as jnp
from jax import lax
from jax.sharding import PartitionSpec as P


def update_step(moments, counts, total_rows):
    width = moments.shape[1] // 2
    denominator = (counts + 1.0)[:, None]
    fresh_means = moments[:, :width] / denominator
    fresh_variances = (moments[:, width:] + 1.0) / denominator - fresh_means * fresh_means + 0.01
    fresh_weights = jnp.log((counts + 1.0) / total_rows)
    return (fresh_means, fresh_variances, fresh_weights)


def on_device(features, means, variances, weight_logits):
    owned_count = means.shape[0]
    width = means.shape[1]
    first_owned = lax.axis_index("comp") * owned_count
    log_weights = lax.dynamic_slice_in_dim(
        jax.nn.log_softmax(weight_logits), first_owned, owned_count
    )
    inverse = 1.0 / variances
    coefficient = jnp.concatenate([-0.5 * inverse, means * inverse], axis=1)
    offsets = (
        log_weights
        - 0.5 * jnp.sum(jnp.log(variances) + means * means * inverse, axis=1)
        - 0.5 * width * math.log(2.0 * math.pi)
    )
    all_coefficient, all_offsets = (
        lax.all_gather(coefficient, "comp", axis=0, tiled=True),
        lax.all_gather(offsets, "comp", axis=0, tiled=True),
    )
    total_comps = all_coefficient.shape[0]
    local_rows = features.shape[0]
    block_size = min(512, local_rows)
    moments = jnp.zeros((total_comps, 2 * width), jnp.float32)
    counts = jnp.zeros((total_comps,), jnp.float32)
    score_pieces = []
    ones_row = jnp.ones((block_size,), jnp.bfloat16)
    for block_index in range(local_rows // block_size):
        block_rows = features[block_index * block_size : (block_index + 1) * block_size]
        values = block_rows.astype(jnp.float32)
        squared = values * values
        scores = (
            jnp.dot(
                jnp.concatenate([squared, values], axis=1),
                all_coefficient.T,
                precision=lax.Precision.HIGHEST,
            )
            + all_offsets
        )
        highest = jnp.max(scores, axis=1, keepdims=True)
        exponent = jnp.exp(scores - highest)
        totals = jnp.sum(exponent, axis=1, keepdims=True)
        responsibility = (exponent / totals).astype(jnp.bfloat16)
        score_pieces.append((highest[:, 0] + jnp.log(totals[:, 0])) / width)
        moment_inputs = jnp.concatenate([block_rows, squared.astype(jnp.bfloat16)], axis=1)
        moments = moments + jnp.dot(
            responsibility.T, moment_inputs, preferred_element_type=jnp.float32
        )
        counts = counts + jnp.dot(ones_row, responsibility, preferred_element_type=jnp.float32)
    row_scores = jnp.concatenate(score_pieces, axis=0)
    total_rows = jnp.float32(
        local_rows * lax.axis_size("grp") * lax.axis_size("comp") + total_comps
    )
    owned_moments, owned_counts = (
        lax.psum_scatter(moments, "comp", scatter_dimension=0, tiled=True),
        lax.psum_scatter(counts, "comp", scatter_dimension=0, tiled=True),
    )
    summed_moments, summed_counts = lax.psum((owned_moments, owned_counts), "grp")
    owned_means, owned_variances, owned_weights = update_step(
        summed_moments, summed_counts, total_rows
    )
    fresh_means, fresh_variances, fresh_weights = (
        lax.all_gather(owned_means, "comp", axis=0, tiled=True),
        lax.all_gather(owned_variances, "comp", axis=0, tiled=True),
        lax.all_gather(owned_weights, "comp", axis=0, tiled=True),
    )
    return (fresh_means, fresh_variances, fresh_weights, row_scores)


def solution(mesh):
    return jax.shard_map(
        on_device,
        mesh=mesh,
        in_specs=(P(("grp", "comp"), None), P("comp", None), P("comp", None), P()),
        out_specs=(P(), P(), P(), P(("grp", "comp"))),
        check_vma=False,
    )
```

profile of v0, /device:TPU:1, one launch (start us, length us, event | category | flops | bytes accessed | tf_op | source)
XLA Modules:
  0.0 667.8 jit_solution(7792017935220275641)
XLA Ops:
  7.2 0.0 all-gather.4.cloned.1.call-start
  7.2 0.9 add_reduce_fusion.4
  8.1 0.6 pad_maximum_fusion
  8.7 0.0 all-gather.4.cloned.1.call-update
  8.7 0.0 reduce-scatter.2.cloned.1.call-start
  8.8 1.3 reduce_max.46
  10.1 1.9 exponential_reduce_fusion
  12.7 1.4 fusion.64
  14.7 1.3 subtract_subtract_fusion
  16.0 0.2 add_dynamic-update-slice_fusion
  16.2 112.2 %all-reduce = f32[1024]{0:T(1024)S(1)} all-reduce(f32[1024]{0:T(1024)S(1)} %add_dynamic-update-slice_fusion), channel_id=1, replica_groups=mesh['grp'=8,'comp'=64] {'comp'}, use_global_device_ids=true, to_apply=%add | all-reduce | flops 1024 | bytes 8192
  128.4 2.3 fusion.63
  130.8 0.0 copy-done.3
  130.8 1.4 fusion.38
  132.2 5.9 all-gather.4.cloned.1.call-done
  138.0 5.5 fusion.4
  143.5 0.0 copy-done
  143.5 0.0 copy-done.4
  143.5 3.6 fusion.12
  147.1 3.7 add_reduce_fusion
  150.8 4.4 fusion.3
  155.3 1.5 fusion.1
  156.8 0.0 copy-start.1
  156.8 0.0 copy-start.8
  156.8 0.0 copy-start.11
  156.9 1.4 divide_convert_fusion.2
  158.2 0.0 copy-done.8
  158.2 0.0 copy-done.11
  158.3 0.0 copy-start.6
  158.3 0.0 copy-start.10
  158.3 0.8 fusion.24
  159.0 0.2 copy-done.6
  159.2 0.1 copy-done.10
  159.3 0.7 fusion.20
  160.0 0.2 copy-done.5
  160.2 0.1 copy-done.9
  160.3 0.7 fusion.28
  161.1 0.0 copy-done.1
  161.1 0.2 copy-done.7
  161.3 2.1 add_add_fusion
  163.4 0.0 reduce-scatter.2.cloned.1.call-update
  163.4 0.0 all-gather.6.cloned.1.call-start
  164.1 0.0 copy-start.2
  164.1 0.2 fusion.49
  164.4 0.2 fusion.47
  164.6 0.3 fusion.45
  164.9 0.5 copy-done.2
  165.3 0.2 fusion.43
  165.6 104.4 %all-reduce.2 = f32[1024]{0:T(1024)S(1)} all-reduce(f32[1024]{0:T(1024)S(1)} %add_add_fusion.1), channel_id=3, replica_groups=mesh['grp'=8,'comp'=64] {'comp'}, use_global_device_ids=true, to_apply=%region_13.14.clone | all-reduce | flops 1024 | bytes 8192
  270.0 0.1 dynamic-slice.3
  270.1 114.1 %reduce-scatter.2.cloned.1.call-done = f32[16,512]{1,0:T(8,128)} async-done(((f32[1024,512]{1,0:T(8,128)}), f32[16,512]{1,0:T(8,128)}) %reduce-scatter.2.cloned.1.call-update) | async-done | bytes 32784 | tf_op jit(solution)/shard_map/reduce_scatter | solution.py:70
  384.2 35.4 %all-reduce.3 = (f32[16,512]{1,0:T(8,128)S(1)}, f32[16]{0:T(128)S(1)}) all-reduce(f32[16,512]{1,0:T(8,128)} %reduce-scatter.2.cloned.1.call-done, f32[16]{0:T(128)S(1)} %dynamic-slice.3), channel_id=1, replica_groups=mesh['grp'=8,'comp'=64] {'grp'}, use_global_device_ids=true, to_apply=%region_12.13 | all-reduce | flops 8208 | bytes 65664 | tf_op jit(solution)/shard_map/psum | solution.py:73
  419.5 0.1 log_dynamic-update-slice_fusion
  419.6 0.7 fusion.41
  420.3 0.0 all-gather.6.cloned.1.call-update
  420.4 0.0 all-gather.8.cloned.1.call-start
  420.4 0.5 all-gather.8.cloned.1.call-update
  421.0 0.6 pad_maximum_fusion.1
  421.6 115.8 %all-reduce.1 = f32[1024]{0:T(1024)} all-reduce(f32[1024]{0:T(1024)S(1)} %get-tuple-element.41), channel_id=1, replica_groups=mesh['grp'=8,'comp'=64] {'comp'}, use_global_device_ids=true, to_apply=%add.1 | all-reduce | flops 1024 | bytes 8192
  537.4 0.8 all-gather.6.cloned.1.call-done
  538.2 119.8 %all-gather.8.cloned.1.call-done = f32[1024,256]{1,0:T(8,128)} async-done(((f32[16,256]{1,0:T(8,128)}), f32[1024,256]{1,0:T(8,128)}) %all-gather.8.cloned.1.call-update) | async-done | bytes 1048592 | tf_op jit(solution)/shard_map/all_gather | solution.py:79
  658.0 2.4 copy.12
  660.3 0.0 copy-done.12
  660.3 1.0 copy.13
  (12 shorter events, 0.0 us)
Async XLA Ops:
  7.2 130.9 %all-gather.4.cloned.1.call-start = ((), (), s32[]{:S(2)}) async-start(), calls=%async_computation.1 | async-start | bytes 2129920 | tf_op jit(solution)/shard_map/all_gather | solution.py:33
  8.7 375.5 %reduce-scatter.2.cloned.1.call-start = ((), (), s32[]{:S(2)}) async-start(), calls=%async_computation.2 | async-start | bytes 2129920 | tf_op jit(solution)/shard_map/reduce_scatter | solution.py:70
  128.4 2.3 copy-start.3
  138.0 5.5 copy-start
  138.0 5.5 copy-start.4
  156.8 4.2 copy-start.1
  156.8 1.4 copy-start.8
  156.8 1.4 copy-start.11
  158.3 1.0 copy-start.6
  158.3 1.0 copy-start.10
  159.3 0.9 copy-start.5
  159.3 1.0 copy-start.9
  160.3 0.9 copy-start.7
  163.4 374.8 %all-gather.6.cloned.1.call-start = ((), (), s32[]{:S(2)}) async-start(), calls=%async_computation.3 | async-start | bytes 1064960 | tf_op jit(solution)/shard_map/all_gather | solution.py:78
  164.1 1.2 copy-start.2
  420.4 237.6 %all-gather.8.cloned.1.call-start = ((), (), s32[]{:S(2)}) async-start(), calls=%async_computation.4 | async-start | bytes 1064960 | tf_op jit(solution)/shard_map/all_gather | solution.py:79
  658.0 2.4 copy-start.12
Sparse Core Ops, SparseCore 0:
  10.2 127.8 all-gather.3
  163.5 220.5 reduce-scatter.1
  420.5 117.6 all-gather.5
  541.0 116.9 all-gather.7
where the time goes:
time: 669 us; the launch traced here: 668 us
  blocking collectives  368 us (55%)
  waiting for transfers between devices  241 us (36%)
  matrix products  22.6 us (3%)
  between operations  15.9 us (2%)
  other arithmetic  14.3 us (2%)
    unnamed x3, blocking collectives  332 us
    all_gather x1, waiting for transfers between devices, on_device(): lax.all_gather(owned_variances, 'comp', axis=0, tiled=True)  120 us
    reduce_scatter x1, waiting for transfers between devices, on_device(): lax.psum_scatter(moments, 'comp', scatter_dimension=0, tiled=True)  114 us
    psum x1, blocking collectives, on_device(): lax.psum((owned_moments, owned_counts), 'grp')  35.4 us
    dot_general x4, matrix products, on_device(): jnp.dot(jnp.concatenate([squared, values], axis=1), all_coefficient.T, pr...  17.2 us
  transfers between devices with their start and end apart: 4, of which 4 were waited for; matrix products, arithmetic and copies ran while one was open for 2% of the time, Pallas kernels for 0%

commit v1 on v0

v1 whole, which is shorter than its diff:
```python
import functools
import math

import jax
import jax.numpy as jnp
from jax import lax
from jax.experimental import pallas as pl
from jax.experimental.pallas import tpu as pltpu
from jax.sharding import PartitionSpec as P

MESH = pl.DeviceIdType.MESH
VMEM = pl.BlockSpec(memory_space=pltpu.VMEM)
BF16 = jnp.bfloat16
F32 = jnp.float32

XA, XB, YA, YB = 0, 1, 2, 3
ORDERS = ((XA, XB, YA, YB), (XB, XA, YB, YA), (YA, YB, XA, XB), (YB, YA, XB, XA))
STREAMS = 4
DEPTH = 16


def chunk_bits(y_hi, y_lo, u, v):
    return ((u + v) % 2, u, (y_hi + y_lo) % 2, y_hi)


def place():
    grp = lax.axis_index("grp")
    comp = lax.axis_index("comp")
    y, u = lax.div(grp, 2), lax.rem(grp, 2)
    v, z, core = lax.div(comp, 32), lax.rem(lax.div(comp, 2), DEPTH), lax.rem(comp, 2)
    y_hi, y_lo = lax.div(y, 2), lax.rem(y, 2)
    bits = (lax.rem(u + v, 2), u, lax.rem(y_hi + y_lo, 2), y_hi)
    flip_v = comp + 32 - 64 * v
    partners = (
        (grp, flip_v),
        (grp + 1 - 2 * u, flip_v),
        (2 * (y + 1 - 2 * y_lo) + u, comp),
        (2 * (3 - y) + u, comp),
    )
    sibling = (grp, comp + 1 - 2 * core)

    def along_z(step):
        return (grp, 32 * v + 2 * lax.rem(z + step, DEPTH) + core)

    return grp, z, core, bits, partners, sibling, along_z


def greet(partners, sibling, along_z):
    barrier = pltpu.get_barrier_semaphore()
    peers = [*partners, sibling, *(along_z(step) for step in range(1, DEPTH))]
    for peer in peers:
        pl.semaphore_signal(barrier, inc=1, device_id=peer, device_id_type=MESH)
    pl.semaphore_wait(barrier, len(peers))


def send(source, target, sems, at, peer):
    copy = pltpu.make_async_remote_copy(
        src_ref=source,
        dst_ref=target,
        send_sem=sems.at[(0, *at)],
        recv_sem=sems.at[(1, *at)],
        device_id=peer,
        device_id_type=MESH,
    )
    copy.start()
    return copy


def gather_kernel(means_ref, variances_ref, out_ref, tiles, arrived, z_sems, plane_sems, core_sems):
    grp, z, core, bits, partners, sibling, along_z = place()
    for index in range(8):
        source = means_ref if index < 4 else variances_ref
        column, row = (index // 2) % 2, index % 2
        tiles[index] = source[row * 8 : row * 8 + 8, column * 128 : column * 128 + 128]
    greet(partners, sibling, along_z)
    copies = [
        send(tiles.at[grp], arrived.at[z], z_sems, (step,), along_z(step))
        for step in range(1, DEPTH)
    ]
    arrived[z] = tiles[grp]
    for copy in copies:
        copy.wait()
    starts = []
    for stream, order in enumerate(ORDERS):
        own = core * 16
        for level, direction in enumerate(order):
            own = own + bits[direction] * (8 >> level)
        starts.append(own)
        for slot in range(4):
            out_ref[stream, own, slot] = arrived[stream * 4 + slot]
    shared = []
    pending = [None] * STREAMS
    for level in range(5):
        for stream, order in enumerate(ORDERS):
            size = 1 << level
            if level > 0:
                pending[stream].wait()
                fresh_bit = bits[order[4 - level]]
                half = size // 2
                fresh = starts[stream] + (1 - 2 * fresh_bit) * half
                starts[stream] = starts[stream] - fresh_bit * half
            else:
                half, fresh = 1, starts[stream]
            if level < 4:
                direction = order[3 - level]
                held = out_ref.at[stream, pl.ds(starts[stream], size)]
                pending[stream] = send(held, held, plane_sems, (level, stream), partners[direction])
            held = out_ref.at[stream, pl.ds(fresh, half)]
            shared.append(send(held, held, core_sems, (level, stream), sibling))
    for copy in shared:
        copy.wait()


def gather(means, variances):
    return pl.pallas_call(
        gather_kernel,
        out_shape=jax.ShapeDtypeStruct((STREAMS, 32, 4, 8, 128), F32),
        in_specs=[VMEM, VMEM],
        out_specs=VMEM,
        scratch_shapes=[
            pltpu.VMEM((8, 8, 128), F32),
            pltpu.VMEM((DEPTH, 8, 128), F32),
            pltpu.SemaphoreType.DMA((2, DEPTH)),
            pltpu.SemaphoreType.DMA((2, 4, STREAMS)),
            pltpu.SemaphoreType.DMA((2, 5, STREAMS)),
        ],
        compiler_params=pltpu.CompilerParams(
            collective_id=0, has_side_effects=True, vmem_limit_bytes=16 << 20
        ),
    )(means, variances)


def stats_kernel(
    parameters_ref, features_ref, logits_ref, moments_ref, counts_ref, rows_ref,
    weights, offsets, inputs, scores, shares, sums,
):
    total_comps, width = 1024, 256
    local_rows = features_ref.shape[0]
    block = 256
    logits = logits_ref[...]
    top = jnp.max(logits)
    log_weights = logits - top - jnp.log(jnp.sum(jnp.exp(logits - top)))
    for piece in range(8):
        spread = jnp.broadcast_to(log_weights[piece : piece + 1, :], (128, 128))
        offsets[piece * 128 : piece * 128 + 128, :] = jnp.transpose(spread)

    for v in range(2):
        for z in range(DEPTH):
            for core in range(2):
                first = 16 * (32 * v + 2 * z + core)
                rows = slice(first, first + 16)
                order = ORDERS[z // 4]

                def table(kind, column):
                    pieces = []
                    for u in range(2):
                        bits = chunk_bits(kind, column, u, v)
                        index = core * 16
                        for level, direction in enumerate(order):
                            index = index + bits[direction] * (8 >> level)
                        pieces.append(parameters_ref[z // 4, index, z % 4])
                    return jnp.concatenate(pieces, axis=0)

                penalty = None
                for column in range(2):
                    mean, variance = table(0, column), table(1, column)
                    inverse = 1.0 / variance
                    square_part = -0.5 * inverse
                    linear_part = mean * inverse
                    term = jnp.log(variance) + mean * linear_part
                    penalty = term if penalty is None else penalty + term
                    square_high = square_part.astype(BF16)
                    square_low = (square_part - square_high.astype(F32)).astype(BF16)
                    linear_high = linear_part.astype(BF16)
                    linear_low = (linear_part - linear_high.astype(F32)).astype(BF16)
                    for place_at, value in enumerate(
                        (square_high, square_high, square_low, linear_high, linear_low)
                    ):
                        at = place_at * width + column * 128
                        weights[rows, at : at + 128] = value
                penalty = jnp.sum(penalty, axis=1, keepdims=True)
                offsets[rows, :] = (
                    offsets[rows, :] - 0.5 * penalty - 0.5 * width * math.log(2.0 * math.pi)
                )

    sums[...] = jnp.zeros_like(sums)

    def visit(step, carry):
        at = pl.multiple_of(step * block, block)
        x = features_ref[pl.ds(at, block), :]
        values = x.astype(F32)
        squared = values * values
        high = squared.astype(BF16)
        low = (squared - high.astype(F32)).astype(BF16)
        inputs[pl.ds(at, block), :width] = x
        inputs[pl.ds(at, block), width:] = high
        right = jnp.concatenate([high, low, high, x, x], axis=1)
        best = None
        for part in range(0, total_comps, 256):
            raw = lax.dot_general(
                weights[part : part + 256, :], right, (((1,), (1,)), ((), ())),
                preferred_element_type=F32,
            )
            offset = offsets[part : part + 256, :]
            raw = raw + jnp.concatenate([offset, offset], axis=1)
            scores[part : part + 256, :] = raw
            here = jnp.max(raw, axis=0, keepdims=True)
            best = here if best is None else jnp.maximum(best, here)
        totals = None
        for part in range(0, total_comps, 256):
            exponent = jnp.exp(scores[part : part + 256, :] - best)
            scores[part : part + 256, :] = exponent
            here = jnp.sum(exponent, axis=0, keepdims=True)
            totals = here if totals is None else totals + here
        rows_ref[:, pl.ds(at, block)] = (best + jnp.log(totals)) / width
        scale = 1.0 / totals
        for part in range(0, total_comps, 256):
            share = (scores[part : part + 256, :] * scale).astype(BF16)
            shares[part : part + 256, pl.ds(at, block)] = share
            rounded = share.astype(F32)
            sums[part : part + 256, :] += rounded[:, :128] + rounded[:, 128:]
        return carry

    lax.fori_loop(0, local_rows // block, visit, 0)
    for part in range(0, total_comps, 256):
        moments_ref[part : part + 256, :] = jnp.dot(
            shares[part : part + 256, :], inputs[...], preferred_element_type=F32
        )
    for piece in range(8):
        turned = jnp.transpose(sums[piece * 128 : piece * 128 + 128, :])
        counts_ref[piece : piece + 1, :] = jnp.sum(turned, axis=0, keepdims=True)


def stats(parameters, features, logits):
    rows = features.shape[0]
    return pl.pallas_call(
        stats_kernel,
        out_shape=(
            jax.ShapeDtypeStruct((1024, 512), F32),
            jax.ShapeDtypeStruct((8, 128), F32),
            jax.ShapeDtypeStruct((1, rows), F32),
        ),
        in_specs=[VMEM] * 3,
        out_specs=(VMEM,) * 3,
        scratch_shapes=[
            pltpu.VMEM((1024, 1280), BF16),
            pltpu.VMEM((1024, 128), F32),
            pltpu.VMEM((rows, 512), BF16),
            pltpu.VMEM((1024, 256), F32),
            pltpu.VMEM((1024, rows), BF16),
            pltpu.VMEM((1024, 128), F32),
        ],
        compiler_params=pltpu.CompilerParams(vmem_limit_bytes=40 << 20),
    )(parameters, features, logits)


def reduce_kernel(
    moments_ref, counts_ref, out_ref, counts_out_ref,
    kept, core_in, in_0, in_1, in_2, in_3, mine, z_in, z_out, counts_z, counts_in, counts_now,
    core_sems, plane_sems, z_sems, back_z_sems, back_plane_sems, back_core_sems,
    counts_z_sems, counts_sems,
):
    grp, z, core, bits, partners, sibling, along_z = place()
    plane_in = (in_0, in_1, in_2, in_3)
    half_comps = 512
    greet(partners, sibling, along_z)
    core_copies = []
    for stream in range(STREAMS):
        source = moments_ref.at[pl.ds((1 - core) * half_comps + stream * 128, 128)]
        core_copies.append(send(source, core_in.at[stream], core_sems, (stream,), sibling))
    counts_copies = [
        send(counts_ref, counts_z.at[z], counts_z_sems, (step,), along_z(step))
        for step in range(1, DEPTH)
    ]
    counts_z[z] = counts_ref[...]

    starts = [[0] * STREAMS]
    pending = [None] * STREAMS

    def advance(level):
        half = 64 >> level
        for stream, order in enumerate(ORDERS):
            start = starts[level][stream]
            bit = bits[order[level]]
            source = kept.at[stream, pl.ds(start + (1 - bit) * half, half)]
            pending[stream] = send(
                source, plane_in[level].at[stream], plane_sems, (level, stream),
                partners[order[level]],
            )

    for stream in range(STREAMS):
        core_copies[stream].wait()
        kept[stream] = (
            moments_ref[pl.ds(core * half_comps + stream * 128, 128), :] + core_in[stream]
        )
    advance(0)
    for copy in counts_copies:
        copy.wait()
    total = counts_z[0]
    for index in range(1, DEPTH):
        total = total + counts_z[index]
    counts_now[0] = total
    routes = (sibling, *partners)

    def count_start(level):
        return send(counts_now.at[level], counts_in.at[level], counts_sems, (level,), routes[level])

    def count_end(level, copy):
        copy.wait()
        counts_now[level + 1] = counts_now[level] + counts_in[level]

    counting = count_start(0)
    for level in range(4):
        half = 64 >> level
        following = []
        for stream, order in enumerate(ORDERS):
            pending[stream].wait()
            keep = starts[level][stream] + bits[order[level]] * half
            kept[stream, pl.ds(keep, half), :] = (
                kept[stream, pl.ds(keep, half), :] + plane_in[level][stream]
            )
            following.append(keep)
        starts.append(following)
        if level < 3:
            advance(level + 1)
        count_end(level, counting)
        counting = count_start(level + 1)
    for stream in range(STREAMS):
        for column in range(4):
            mine[stream * 4 + column] = kept[
                stream, pl.ds(starts[4][stream], 8), column * 128 : column * 128 + 128
            ]
    copies = [
        send(mine.at[lax.rem(z + step, DEPTH)], z_in.at[step], z_sems, (step,), along_z(step))
        for step in range(1, DEPTH)
    ]
    count_end(4, counting)
    counts_out_ref[...] = counts_now[5]
    tile = mine[z]
    for step, copy in enumerate(copies):
        copy.wait()
        tile = tile + z_in[step + 1]
    z_out[z] = tile
    copies = [
        send(z_out.at[z], z_out.at[z], back_z_sems, (step,), along_z(step))
        for step in range(1, DEPTH)
    ]
    for copy in copies:
        copy.wait()
    for stream in range(STREAMS):
        first = core * half_comps + stream * 128 + starts[4][stream]
        for column in range(4):
            out_ref[pl.ds(first, 8), column * 128 : column * 128 + 128] = z_out[stream * 4 + column]
    shared = []
    for level in range(4, -1, -1):
        size = 128 >> level
        for stream, order in enumerate(ORDERS):
            base = core * half_comps + stream * 128
            if level < 4:
                pending[stream].wait()
                fresh = starts[level][stream] + (1 - bits[order[level]]) * (size // 2)
                fresh_size = size // 2
            else:
                fresh, fresh_size = starts[4][stream], size
            if level > 0:
                held = out_ref.at[pl.ds(base + starts[level][stream], size)]
                pending[stream] = send(
                    held, held, back_plane_sems, (level - 1, stream), partners[order[level - 1]]
                )
            held = out_ref.at[pl.ds(base + fresh, fresh_size)]
            shared.append(send(held, held, back_core_sems, (level, stream), sibling))
    for copy in shared:
        copy.wait()


def reduce_all(moments, counts):
    dma = pltpu.SemaphoreType.DMA
    return pl.pallas_call(
        reduce_kernel,
        out_shape=(
            jax.ShapeDtypeStruct((1024, 512), F32),
            jax.ShapeDtypeStruct((8, 128), F32),
        ),
        in_specs=[VMEM, VMEM],
        out_specs=(VMEM, VMEM),
        scratch_shapes=[
            pltpu.VMEM((STREAMS, 128, 512), F32),
            pltpu.VMEM((STREAMS, 128, 512), F32),
            pltpu.VMEM((STREAMS, 64, 512), F32),
            pltpu.VMEM((STREAMS, 32, 512), F32),
            pltpu.VMEM((STREAMS, 16, 512), F32),
            pltpu.VMEM((STREAMS, 8, 512), F32),
            pltpu.VMEM((DEPTH, 8, 128), F32),
            pltpu.VMEM((DEPTH, 8, 128), F32),
            pltpu.VMEM((DEPTH, 8, 128), F32),
            pltpu.VMEM((DEPTH, 8, 128), F32),
            pltpu.VMEM((5, 8, 128), F32),
            pltpu.VMEM((6, 8, 128), F32),
            dma((2, STREAMS)),
            dma((2, 4, STREAMS)),
            dma((2, DEPTH)),
            dma((2, DEPTH)),
            dma((2, 4, STREAMS)),
            dma((2, 5, STREAMS)),
            dma((2, DEPTH)),
            dma((2, 5)),
        ],
        compiler_params=pltpu.CompilerParams(
            collective_id=1, has_side_effects=True, vmem_limit_bytes=24 << 20
        ),
    )(moments, counts)


def update_step(moments, counts, total_rows):
    width = moments.shape[1] // 2
    denominator = (counts + 1.0)[:, None]
    fresh_means = moments[:, :width] / denominator
    fresh_variances = (moments[:, width:] + 1.0) / denominator - fresh_means * fresh_means + 0.01
    fresh_weights = jnp.log((counts + 1.0) / total_rows)
    return (fresh_means, fresh_variances, fresh_weights)


def on_device(features, means, variances, weight_logits):
    parameters = gather(means, variances)
    moments, counts, row_scores = stats(parameters, features, weight_logits.reshape(8, 128))
    moments, counts = reduce_all(moments, counts)
    total_comps = moments.shape[0]
    total_rows = jnp.float32(
        features.shape[0] * lax.axis_size("grp") * lax.axis_size("comp") + total_comps
    )
    fresh = update_step(moments, counts.reshape(total_comps), total_rows)
    return (*fresh, row_scores.reshape(features.shape[0]))


def solution(mesh):
    return jax.shard_map(
        on_device,
        mesh=mesh,
        in_specs=(P(("grp", "comp"), None), P("comp", None), P("comp", None), P()),
        out_specs=(P(), P(), P(), P(("grp", "comp"))),
        check_vma=False,
    )
```

time: 669 us -> 124 us (0.19)
  blocking collectives: 368 us -> 0 us
  waiting for transfers between devices: 241 us -> 0 us
  Pallas kernels: 0 us -> 119 us
  matrix products: 22.6 us -> 0 us
  between operations: 15.9 us -> 0.69 us
  other arithmetic: 14.3 us -> 2.22 us
    unnamed x3 -> x0, blocking collectives: 332 us -> none
    all_gather x3 -> x0, waiting for transfers between devices: 126 us -> none  [the longest x1 120 us: on_device(): lax.all_gather(owned_variances, 'comp', axis=0, tiled=True)]
    pallas_call x0 -> x3, Pallas kernels: none -> 119 us  [the longest x1 64.1 us: reduce_all(): pl.pallas_call(reduce_kernel, out_shape=(jax.ShapeDtypeStruct((1024, 512)...]
    reduce_scatter x1 -> x0, waiting for transfers between devices: 114 us -> none  [on_device(): lax.psum_scatter(moments, 'comp', scatter_dimension=0, tiled=True)]
    psum x1 -> x0, blocking collectives: 35.4 us -> none  [on_device(): lax.psum((owned_moments, owned_counts), 'grp')]
    dot_general x12 -> x0, matrix products: 22.6 us -> none  [the longest x4 17.2 us: on_device(): jnp.dot(jnp.concatenate([squared, values], axis=1), all_coefficient.T, pr...]
  transfers between devices with their start and end apart: 4 -> 0, of which waited for: 4 -> 0; matrix products, arithmetic and copies ran while one was open for 2% -> 0% of each run, Pallas kernels for 0% -> 0%
where the time goes in v1:
time: 124 us; the launch traced here: 123 us
  Pallas kernels  119 us (96%)
  other arithmetic  2.22 us (2%)
  local copies, waits for them, and re-layouts  1.52 us (1%)
    pallas_call x1, Pallas kernels, reduce_all(): pl.pallas_call(reduce_kernel, out_shape=(jax.ShapeDtypeStruct((1024, 512)...  64.1 us
    pallas_call x1, Pallas kernels, gather(): pl.pallas_call(gather_kernel, out_shape=jax.ShapeDtypeStruct((STREAMS, 32...  41.5 us
    pallas_call x1, Pallas kernels, stats(): pl.pallas_call(stats_kernel, out_shape=(jax.ShapeDtypeStruct((1024, 512),...  13.5 us

profile of v1, /device:TPU:1, one launch (start us, length us, event | category | flops | bytes accessed | tf_op | source)
XLA Modules:
  0.0 123.5 jit_solution(6943982880894186374)
XLA Ops:
  0.6 0.0 copy-start
  0.6 0.0 copy-start.1
  0.7 0.8 copy-done.1
  1.4 0.0 copy-start.2
  1.4 0.7 copy-done.2
  2.2 0.0 copy-start.3
  2.2 41.5 %shard_map.75.parameters_ref = f32[4,32,4,8,128]{4,3,2,1,0:T(8,128)S(1)} custom-call(f32[16,256]{1,0:T(8,128)S(1)} %copy-done.1, f32[16,256]{1,0:T(8,128)S(1)} %copy-done.2), custom_call_target="tpu_custom_call" | custom-call | tf_op jit(solution)/shard_map/pallas_call | solution.py:115
  43.7 0.0 copy-done
  43.7 0.0 copy-done.3
  43.7 13.5 %shard_map.76 = (f32[1024,512]{1,0:T(8,128)S(1)}, f32[8,128]{1,0:T(8,128)S(1)}, f32[1,2048]{1,0:T(1,128)}) custom-call(f32[4,32,4,8,128]{4,3,2,1,0:T(8,128)S(1)} %shard_map.75.parameters_ref, bf16[2048,256]{1,0:T(8,128)(2,1)S(1)} %copy-done, f32[8,128]{1,0:T(8,128)S(1)} %bitcast.6), custom_call_target="tpu_custom_call" | custom-call | tf_op jit(solution)/shard_map/pallas_call | solution.py:236
  57.2 64.1 %shard_map.77 = (f32[1024,512]{1,0:T(8,128)S(1)}, f32[8,128]{1,0:T(8,128)S(1)}) custom-call(f32[1024,512]{1,0:T(8,128)S(1)} %get-tuple-element.9.moments_ref, f32[8,128]{1,0:T(8,128)S(1)} %get-tuple-element.10.counts_ref), custom_call_target="tpu_custom_call" | custom-call | tf_op jit(solution)/shard_map/pallas_call | solution.py:378
  121.3 0.6 multiply_log_fusion
  121.9 1.6 %subtract_add_fusion = (f32[1024,256]{1,0:T(8,128)}, f32[1024,256]{1,0:T(8,128)}) fusion(f32[1024,512]{1,0:T(8,128)S(1)} %get-tuple-element.11, f32[1024]{0:T(1024)S(1)} %add_bitcast_fusion), kind=kLoop, calls=%fused_computation | loop fusion | flops 1572864 | bytes 4198400 | tf_op jit(solution)/shard_map/add | solution.py:418
  (1 shorter events, 0.0 us)
Async XLA Ops:
  0.6 43.0 %copy-start = (bf16[2048,256]{1,0:T(8,128)(2,1)S(1)}, bf16[2048,256]{1,0:T(8,128)(2,1)}, u32[]{:S(2)}) copy-start(bf16[2048,256]{1,0:T(8,128)(2,1)} %features_ref.1) | copy-start | bytes 3145732
  0.6 0.8 copy-start.1
  1.4 0.7 copy-start.2
  2.2 41.5 %copy-start.3 = (f32[1024]{0:T(1024)S(1)}, f32[1024]{0:T(1024)}, u32[]{:S(2)}) copy-start(f32[1024]{0:T(1024)} %param.7) | copy-start | bytes 12292

commit v2 on v0

v2 whole, which is shorter than its diff:
```python
import math

import jax
import jax.numpy as jnp
from jax import lax
from jax.experimental import pallas as pl
from jax.experimental.pallas import tpu as pltpu
from jax.sharding import PartitionSpec as P

MESH = pl.DeviceIdType.MESH
BF16 = jnp.bfloat16
F32 = jnp.float32

COMPS, WIDTH = 1024, 256
DEPTH = 16
OFFSETS = sorted(
    ((dx, dy) for dx in range(4) for dy in range(4) if (dx, dy) != (0, 0)),
    key=lambda d: (min(d[0], 4 - d[0]) + min(d[1], 4 - d[1]), d),
)
PEERS = len(OFFSETS)
SHIFTS = (0, 1, 3, 2)
GROUPS = len(SHIFTS)
FAR_FIRST = (3, 1, 2, 0)
BLOCK = 256


class Place:
    def __init__(self):
        self.grp = lax.axis_index("grp")
        comp = lax.axis_index("comp")
        y, u = lax.div(self.grp, 2), lax.rem(self.grp, 2)
        v, rest = lax.div(comp, 32), lax.rem(comp, 32)
        self.z, self.core = lax.div(rest, 2), lax.rem(rest, 2)
        self.block, self.slot = lax.div(self.z, 4), lax.rem(self.z, 4)
        self.chip = 2 * self.grp + v
        self.sibling = (self.grp, comp + 1 - 2 * self.core)
        self.base = 32 * v + self.core
        x = 2 * u + v
        self.plane = []
        for dx, dy in OFFSETS:
            across, along = lax.rem(x + dx, 4), lax.rem(y + dy, 4)
            grp = 2 * along + lax.div(across, 2)
            side = lax.rem(across, 2)
            self.plane.append(((grp, 32 * side + rest), 2 * grp + side))

    def at_z(self, z):
        return (self.grp, self.base + 2 * z)

    def group(self, index):
        return lax.rem(self.block + SHIFTS[index], 4)


def remote(source, target, send_sem, recv_sem, peer):
    return pltpu.make_async_remote_copy(
        src_ref=source, dst_ref=target, send_sem=send_sem, recv_sem=recv_sem,
        device_id=peer, device_id_type=MESH,
    )


def await_bytes(ref, sem):
    pltpu.make_async_copy(ref, ref, sem).wait()


def kernel(
    features_hbm, means_hbm, variances_hbm, logits_ref,
    moments_ref, counts_ref, rows_ref,
    features, means, variances, tiles, arrived, table, weights, log_weights, inputs,
    exponents, peaks, totals, shares, tally,
    core_out, core_in, own, plane_in, z_out, z_in, back, spread,
    counts_z, counts_plane, counts_pair,
    load_sems, z_send, z_recv, plane_send, plane_recv, pair_send, pair_recv,
    rz_send, rz_recv, rplane_send, rplane_recv, rpair_send, rpair_recv,
    bz_send, bz_recv, bplane_send, bplane_recv, bpair_send, bpair_recv,
    count_send, count_recv,
):
    me = Place()
    local_rows = features.shape[0]
    loads = [
        pltpu.make_async_copy(source, target, load_sems.at[index])
        for index, (source, target) in enumerate(
            ((means_hbm, means), (variances_hbm, variances), (features_hbm, features))
        )
    ]
    for load in loads:
        load.start()
    barrier = pltpu.get_barrier_semaphore()
    greeted = [me.at_z(lax.rem(me.z + step, DEPTH)) for step in range(1, DEPTH)]
    greeted += [peer for peer, _ in me.plane] + [me.sibling]
    for peer in greeted:
        pl.semaphore_signal(barrier, inc=1, device_id=peer, device_id_type=MESH)
    loads[0].wait()
    loads[1].wait()
    for index in range(8):
        source = means if index < 4 else variances
        column, row = (index // 2) % 2, index % 2
        tiles[index] = source[row * 8 : row * 8 + 8, column * 128 : column * 128 + 128]
    arrived[me.z] = tiles[me.grp]
    pl.semaphore_wait(barrier, len(greeted))

    z_steps = (8, 7, 9, 6, 10, 5, 11, 4, 12, 3, 13, 2, 14, 1, 15)
    for step in z_steps:
        remote(
            tiles.at[me.grp], arrived.at[me.z], z_send.at[0], z_recv.at[me.block],
            me.at_z(lax.rem(me.z + step, DEPTH)),
        ).start()

    logits = logits_ref[...]
    top = jnp.max(logits)
    normal = logits - top - jnp.log(jnp.sum(jnp.exp(logits - top)))
    for piece in range(8):
        wide = jnp.broadcast_to(normal[piece : piece + 1, :], (128, 128))
        log_weights[piece * 128 : piece * 128 + 128, :] = jnp.transpose(wide)
    loads[2].wait()

    def prepare(step, carry):
        at = pl.multiple_of(step * 128, 128)
        x = features[pl.ds(at, 128), :]
        values = x.astype(F32)
        squared = values * values
        high = squared.astype(BF16)
        low = (squared - high.astype(F32)).astype(BF16)
        for index, value in enumerate((high, low, high, x, x)):
            inputs[pl.ds(at, 128), index * WIDTH : index * WIDTH + WIDTH] = value
        return carry

    lax.fori_loop(0, local_rows // 128, prepare, 0)

    def await_group(buffer, sems, index):
        count = 3 if index == 0 else 4
        await_bytes(buffer.at[pl.ds(0, count)], sems.at[me.group(index)])

    for index in range(GROUPS):
        await_group(arrived, z_recv, index)
        first = 4 * me.group(index)
        table[index, me.core, me.chip] = arrived[pl.ds(first, 4)]
        for offset, (peer, _) in enumerate(me.plane):
            remote(
                arrived.at[pl.ds(first, 4)], table.at[index, me.core, me.chip],
                plane_send.at[index], plane_recv.at[index], peer,
            ).start()

    def pair_copy(index):
        part = table.at[index, me.core]
        return remote(part, part, pair_send.at[index], pair_recv.at[index], me.sibling)

    def make_weights(index):
        natural = 128 * me.group(index)
        for v in range(2):
            for j in range(4):
                for h in range(2):
                    def load(kind, column):
                        chips = [2 * (4 * kind + 2 * column + r) + v for r in range(2)]
                        return jnp.concatenate([table[index, h, chip, j] for chip in chips], axis=0)

                    inner = 32 * j + 16 * h
                    row = 128 * v + inner
                    rows = slice(row, row + 16)
                    penalty = None
                    for column in range(2):
                        mean, variance = load(0, column), load(1, column)
                        inverse = 1.0 / variance
                        square_part = -0.5 * inverse
                        linear_part = mean * inverse
                        term = jnp.log(variance) + mean * linear_part
                        penalty = term if penalty is None else penalty + term
                        square_high = square_part.astype(BF16)
                        square_low = (square_part - square_high.astype(F32)).astype(BF16)
                        linear_high = linear_part.astype(BF16)
                        linear_low = (linear_part - linear_high.astype(F32)).astype(BF16)
                        for at, value in enumerate(
                            (square_high, square_high, square_low, linear_high, linear_low)
                        ):
                            at = at * WIDTH + column * 128
                            weights[index, rows, at : at + 128] = value
                    penalty = jnp.sum(penalty, axis=1, keepdims=True)
                    here = pl.ds(pl.multiple_of(512 * v + natural + inner, 16), 16)
                    log_weights[here, :] = (
                        log_weights[here, :] - 0.5 * penalty - 0.5 * WIDTH * math.log(2.0 * math.pi)
                    )

    def make_scores(index):
        natural = 128 * me.group(index)

        def visit(step, carry):
            at = pl.multiple_of(step * BLOCK, BLOCK)
            right = inputs[pl.ds(at, BLOCK), :]
            raws = []
            for v in range(2):
                raw = lax.dot_general(
                    weights[index, v * 128 : v * 128 + 128, :], right, (((1,), (1,)), ((), ())),
                    preferred_element_type=F32,
                )
                offset = log_weights[pl.ds(pl.multiple_of(512 * v + natural, 128), 128), :]
                raws.append(raw + jnp.concatenate([offset] * (BLOCK // 128), axis=1))
            best = jnp.max(jnp.maximum(raws[0], raws[1]), axis=0, keepdims=True)
            total = None
            for v in range(2):
                value = jnp.exp(raws[v] - best)
                exponents[index, v, :, pl.ds(at, BLOCK)] = value
                total = value if total is None else total + value
            peaks[index : index + 1, pl.ds(at, BLOCK)] = best
            totals[index : index + 1, pl.ds(at, BLOCK)] = jnp.sum(total, axis=0, keepdims=True)
            return carry

        lax.fori_loop(0, local_rows // BLOCK, visit, 0)

    for index in range(GROUPS):
        await_bytes(table.at[index, 0, pl.ds(0, PEERS)], plane_recv.at[index])
        copy = pair_copy(index)
        copy.start()
        copy.wait_recv()
        make_weights(index)
        make_scores(index)

    best = jnp.max(peaks[0:GROUPS, :], axis=0, keepdims=True)
    factors = jnp.exp(peaks[0:GROUPS, :] - best)
    total = jnp.sum(totals[0:GROUPS, :] * factors, axis=0, keepdims=True)
    rows_ref[...] = (best + jnp.log(total)) / WIDTH
    totals[0:GROUPS, :] = factors / total

    def rpair_copy(index):
        return remote(
            core_out.at[index], core_in.at[index], rpair_send.at[index], rpair_recv.at[index],
            me.sibling,
        )

    for index in FAR_FIRST:
        def share(step, sums):
            at = pl.multiple_of(step * BLOCK, BLOCK)
            scale = totals[index : index + 1, pl.ds(at, BLOCK)]
            following = []
            for v in range(2):
                rounded = (exponents[index, v, :, pl.ds(at, BLOCK)] * scale).astype(BF16)
                shares[index, v, :, pl.ds(at, BLOCK)] = rounded
                wide = rounded.astype(F32)
                tally[v] += wide[:, :128] + wide[:, 128:]
            return sums

        tally[...] = jnp.zeros_like(tally)
        lax.fori_loop(0, local_rows // BLOCK, share, 0)
        for v in range(2):
            line = jnp.sum(jnp.transpose(tally[v]), axis=0, keepdims=True)
            counts_pair[0, pl.ds(4 * v + me.group(index), 1), :] = line
        for target, half in ((core_out, 1 - me.core), (own, me.core)):
            result = jnp.dot(
                shares[index, half], inputs[:, 2 * WIDTH : 4 * WIDTH], preferred_element_type=F32
            )
            for chip in range(16):
                for j in range(4):
                    target[index, chip, j] = result[
                        chip * 8 : chip * 8 + 8, j * 128 : j * 128 + 128
                    ]
            if target is core_out:
                rpair_copy(index).start()
        rpair_copy(index).wait_recv()
        own[index] = own[index] + core_in[index]
        for offset, (peer, chip) in enumerate(me.plane):
            remote(
                own.at[index, chip], plane_in.at[index, offset],
                rplane_send.at[index], rplane_recv.at[index], peer,
            ).start()

    for step in z_steps:
        remote(
            counts_pair.at[0], counts_z.at[me.z], count_send.at[0], count_recv.at[0],
            me.at_z(lax.rem(me.z + step, DEPTH)),
        ).start()
    counts_z[me.z] = counts_pair[0]

    for index in FAR_FIRST:
        await_bytes(plane_in.at[index], rplane_recv.at[index])
        reduced = own[index, me.chip]
        for offset in range(PEERS):
            reduced = reduced + plane_in[index, offset]
        z_out[index] = reduced
        for step in range(1 if index == 0 else 0, 4):
            slot = lax.rem(me.slot + step, 4)
            remote(
                z_out.at[index, slot], z_in.at[me.z], rz_send.at[0], rz_recv.at[0],
                me.at_z(4 * me.group(index) + slot),
            ).start()
    z_in[me.z] = z_out[0, me.slot]

    await_bytes(counts_z.at[pl.ds(0, DEPTH - 1)], count_recv.at[0])
    counted = counts_z[0]
    for index in range(1, DEPTH):
        counted = counted + counts_z[index]
    counts_plane[me.chip] = counted
    for peer, _ in me.plane:
        remote(
            counts_plane.at[me.chip], counts_plane.at[me.chip], count_send.at[1], count_recv.at[1],
            peer,
        ).start()

    await_bytes(z_in.at[pl.ds(0, DEPTH - 1)], rz_recv.at[0])
    final = z_in[0]
    for index in range(1, DEPTH):
        final = final + z_in[index]
    back[me.z] = final
    for step in z_steps:
        remote(
            back.at[me.z], back.at[me.z], bz_send.at[0], bz_recv.at[me.block],
            me.at_z(lax.rem(me.z + step, DEPTH)),
        ).start()

    await_bytes(counts_plane.at[pl.ds(0, PEERS)], count_recv.at[1])
    counted = counts_plane[0]
    for index in range(1, 16):
        counted = counted + counts_plane[index]
    counts_pair[1] = counted
    pair = remote(
        counts_pair.at[1], counts_pair.at[2], count_send.at[2], count_recv.at[2], me.sibling
    )
    pair.start()

    for index in range(GROUPS):
        await_group(back, bz_recv, index)
        first = 4 * me.group(index)
        spread[index, me.core, me.chip] = back[pl.ds(first, 4)]
        for peer, _ in me.plane:
            remote(
                back.at[pl.ds(first, 4)], spread.at[index, me.core, me.chip],
                bplane_send.at[index], bplane_recv.at[index], peer,
            ).start()

    pair.wait()
    counts_ref[...] = counts_pair[1] + counts_pair[2]

    await_bytes(arrived.at[pl.ds(0, DEPTH - 1)], z_send.at[0])
    await_bytes(counts_z.at[pl.ds(0, DEPTH - 1)], count_send.at[0])
    await_bytes(counts_z.at[pl.ds(0, DEPTH - 1)], count_send.at[1])
    await_bytes(z_in.at[pl.ds(0, DEPTH - 1)], rz_send.at[0])
    await_bytes(z_in.at[pl.ds(0, DEPTH - 1)], bz_send.at[0])
    for index in range(GROUPS):
        await_bytes(plane_in.at[index], plane_send.at[index])
        await_bytes(plane_in.at[index], rplane_send.at[index])
        pair_copy(index).wait_send()
        rpair_copy(index).wait_send()

    def bpair_copy(index):
        part = spread.at[index, me.core]
        return remote(part, part, bpair_send.at[index], bpair_recv.at[index], me.sibling)

    for index in range(GROUPS):
        await_bytes(spread.at[index, 0, pl.ds(0, PEERS)], bplane_recv.at[index])
        bpair_copy(index).start()
    for index in range(GROUPS):
        bpair_copy(index).wait_recv()
        natural = 128 * me.group(index)
        for h in range(2):
            for chip in range(16):
                here = pl.ds(pl.multiple_of(512 * h + natural + 8 * chip, 8), 8)
                for j in range(4):
                    moments_ref[here, j * 128 : j * 128 + 128] = spread[index, h, chip, j]
    for index in range(GROUPS):
        await_bytes(plane_in.at[index], bplane_send.at[index])
        bpair_copy(index).wait_send()


def iterate(features, means, variances, logits):
    rows = features.shape[0]
    dma = pltpu.SemaphoreType.DMA
    hbm = pl.BlockSpec(memory_space=pl.ANY)
    vmem = pl.BlockSpec(memory_space=pltpu.VMEM)
    tile = (8, 128)
    return pl.pallas_call(
        kernel,
        out_shape=(
            jax.ShapeDtypeStruct((COMPS, 2 * WIDTH), F32),
            jax.ShapeDtypeStruct(tile, F32),
            jax.ShapeDtypeStruct((1, rows), F32),
        ),
        in_specs=[hbm, hbm, hbm, vmem],
        out_specs=(vmem,) * 3,
        scratch_shapes=[
            pltpu.VMEM((rows, WIDTH), BF16),
            pltpu.VMEM((16, WIDTH), F32),
            pltpu.VMEM((16, WIDTH), F32),
            pltpu.VMEM((8, *tile), F32),
            pltpu.VMEM((DEPTH, *tile), F32),
            pltpu.VMEM((GROUPS, 2, 16, 4, *tile), F32),
            pltpu.VMEM((GROUPS, 256, 5 * WIDTH), BF16),
            pltpu.VMEM((COMPS, 128), F32),
            pltpu.VMEM((rows, 5 * WIDTH), BF16),
            pltpu.VMEM((GROUPS, 2, 128, rows), F32),
            pltpu.VMEM((8, rows), F32),
            pltpu.VMEM((8, rows), F32),
            pltpu.VMEM((GROUPS, 2, 128, rows), BF16),
            pltpu.VMEM((2, 128, 128), F32),
            pltpu.VMEM((GROUPS, 16, 4, *tile), F32),
            pltpu.VMEM((GROUPS, 16, 4, *tile), F32),
            pltpu.VMEM((GROUPS, 16, 4, *tile), F32),
            pltpu.VMEM((GROUPS, PEERS, 4, *tile), F32),
            pltpu.VMEM((GROUPS, 4, *tile), F32),
            pltpu.VMEM((DEPTH, *tile), F32),
            pltpu.VMEM((DEPTH, *tile), F32),
            pltpu.VMEM((GROUPS, 2, 16, 4, *tile), F32),
            pltpu.VMEM((DEPTH, *tile), F32),
            pltpu.VMEM((16, *tile), F32),
            pltpu.VMEM((3, *tile), F32),
            dma((3,)),
            dma((1,)), dma((4,)), dma((4,)), dma((4,)), dma((4,)), dma((4,)),
            dma((1,)), dma((1,)), dma((4,)), dma((4,)), dma((4,)), dma((4,)),
            dma((1,)), dma((4,)), dma((4,)), dma((4,)), dma((4,)), dma((4,)),
            dma((3,)), dma((3,)),
        ],
        compiler_params=pltpu.CompilerParams(
            collective_id=0, has_side_effects=True, vmem_limit_bytes=56 << 20
        ),
    )(features, means, variances, logits)


def update_step(squares, linears, counts, total_rows):
    denominator = (counts + 1.0)[:, None]
    fresh_means = linears / denominator
    fresh_variances = (squares + 1.0) / denominator - fresh_means * fresh_means + 0.01
    fresh_weights = jnp.log((counts + 1.0) / total_rows)
    return (fresh_means, fresh_variances, fresh_weights)


def on_device(features, means, variances, weight_logits):
    moments, counts, row_scores = iterate(
        features, means, variances, weight_logits.reshape(8, 128)
    )
    total_rows = jnp.float32(
        features.shape[0] * lax.axis_size("grp") * lax.axis_size("comp") + COMPS
    )
    fresh = update_step(
        moments[:, :WIDTH], moments[:, WIDTH:], counts.reshape(COMPS), total_rows
    )
    return (*fresh, row_scores.reshape(features.shape[0]))


def solution(mesh):
    return jax.shard_map(
        on_device,
        mesh=mesh,
        in_specs=(P(("grp", "comp"), None), P("comp", None), P("comp", None), P()),
        out_specs=(P(), P(), P(), P(("grp", "comp"))),
        check_vma=False,
    )
```

time: 669 us -> 106 us (0.16)
  blocking collectives: 368 us -> 0 us
  waiting for transfers between devices: 241 us -> 0 us
  Pallas kernels: 0 us -> 99 us
  matrix products: 22.6 us -> 0 us
  between operations: 15.9 us -> 0.64 us
  other arithmetic: 14.3 us -> 5.13 us
    unnamed x3 -> x0, blocking collectives: 332 us -> none
    all_gather x3 -> x0, waiting for transfers between devices: 126 us -> none  [the longest x1 120 us: on_device(): lax.all_gather(owned_variances, 'comp', axis=0, tiled=True)]
    reduce_scatter x1 -> x0, waiting for transfers between devices: 114 us -> none  [on_device(): lax.psum_scatter(moments, 'comp', scatter_dimension=0, tiled=True)]
    pallas_call x0 -> x1, Pallas kernels: none -> 99 us  [iterate(): pl.pallas_call(kernel, out_shape=(jax.ShapeDtypeStruct((COMPS, 2 * WIDTH)...]
    psum x1 -> x0, blocking collectives: 35.4 us -> none  [on_device(): lax.psum((owned_moments, owned_counts), 'grp')]
    dot_general x12 -> x0, matrix products: 22.6 us -> none  [the longest x4 17.2 us: on_device(): jnp.dot(jnp.concatenate([squared, values], axis=1), all_coefficient.T, pr...]
  transfers between devices with their start and end apart: 4 -> 0, of which waited for: 4 -> 0; matrix products, arithmetic and copies ran while one was open for 2% -> 0% of each run, Pallas kernels for 0% -> 0%
where the time goes in v2:
time: 106 us; the launch traced here: 105 us
  Pallas kernels  99 us (93%)
  other arithmetic  5.13 us (5%)
    pallas_call x1, Pallas kernels, iterate(): pl.pallas_call(kernel, out_shape=(jax.ShapeDtypeStruct((COMPS, 2 * WIDTH)...  99 us
    add x1, other arithmetic, update_step(): (squares + 1.0) / denominator - fresh_means * fresh_means + 0.01  3.16 us

profile of v2, /device:TPU:1, one launch (start us, length us, event | category | flops | bytes accessed | tf_op | source)
XLA Modules:
  0.0 105.3 jit_solution(16637504519313743753)
XLA Ops:
  0.6 99.0 %shard_map.75 = (f32[1024,512]{1,0:T(8,128)}, f32[8,128]{1,0:T(8,128)}, f32[1,2048]{1,0:T(1,128)}) custom-call(bf16[2048,256]{1,0:T(8,128)(2,1)} %features_hbm.1, f32[16,256]{1,0:T(8,128)} %means_hbm.1, f32[16,256]{1,0:T(8,128)} %variances_hbm.1, f32[8,128]{1,0:T(8,128)} %bitcast.7), custom_call_target="tpu_custom_call" | custom-call | tf_op jit(solution)/shard_map/pallas_call | solution.py:366
  99.6 1.3 %multiply_log_fusion = f32[1024]{0:T(1024)} fusion(f32[8,128]{1,0:T(8,128)} %get-tuple-element.8), kind=kLoop, calls=%fused_computation.2 | loop fusion | flops 2048 | bytes 8192 | tf_op jit(solution)/shard_map/log | solution.py:417
  100.9 0.7 add_bitcast_fusion
  101.6 0.0 copy-start
  101.6 3.2 %subtract_add_fusion = (f32[1024,256]{1,0:T(8,128)}, f32[1024,256]{1,0:T(8,128)}) fusion(f32[1024,512]{1,0:T(8,128)} %get-tuple-element.7, f32[1024]{0:T(1024)S(1)} %add_bitcast_fusion), kind=kLoop, calls=%fused_computation | loop fusion | flops 1572864 | bytes 4198400 | tf_op jit(solution)/shard_map/add | solution.py:416
  104.7 0.0 copy-done
  104.7 0.6 copy.9
Async XLA Ops:
  101.6 3.2 %copy-start = (f32[1,2048]{1,0:T(1,128)S(1)}, f32[1,2048]{1,0:T(1,128)}, u32[]{:S(2)}) copy-start(f32[1,2048]{1,0:T(1,128)} %get-tuple-element.9) | copy-start | bytes 24580

commit v3 on v2

v3 whole, which is shorter than its diff:
```python
import functools
import math

import jax
import jax.numpy as jnp
from jax import lax
from jax.experimental import pallas as pl
from jax.experimental.pallas import tpu as pltpu
from jax.sharding import PartitionSpec as P

MESH = pl.DeviceIdType.MESH
BF16 = jnp.bfloat16
F32 = jnp.float32

COMPS, WIDTH = 1024, 256
DEPTH = 16
OFFSETS = sorted(
    ((dx, dy) for dx in range(4) for dy in range(4) if (dx, dy) != (0, 0)),
    key=lambda d: (min(d[0], 4 - d[0]) + min(d[1], 4 - d[1]), d),
)
PEERS = len(OFFSETS)
NEAR = (0, 1, -1, 2, -2, 3, -3, 4, -4, 5, -5, 6, -6, 7, -7, 8)
SLOT = {step % DEPTH: slot for slot, step in enumerate(NEAR)}
HOPS = ((0, 1), (1, 3), (4, 2), (6, 2), (8, 2), (10, 2), (12, 2), (14, 2))
HOP_OF = {first + k: hop for hop, (first, count) in enumerate(HOPS) for k in range(count)}
GROUPS = 4
BLOCK = 256


class Place:
    def __init__(self):
        self.grp = lax.axis_index("grp")
        comp = lax.axis_index("comp")
        y, u = lax.div(self.grp, 2), lax.rem(self.grp, 2)
        v, rest = lax.div(comp, 32), lax.rem(comp, 32)
        self.z, self.core = lax.div(rest, 2), lax.rem(rest, 2)
        self.chip = 2 * self.grp + v
        self.sibling = (self.grp, comp + 1 - 2 * self.core)
        self.base = 32 * v + self.core
        x = 2 * u + v
        self.plane = []
        for dx, dy in OFFSETS:
            across, along = lax.rem(x + dx, 4), lax.rem(y + dy, 4)
            grp = 2 * along + lax.div(across, 2)
            side = lax.rem(across, 2)
            self.plane.append(((grp, 32 * side + rest), 2 * grp + side))

    def z_of(self, slot):
        return lax.rem(self.z + NEAR[slot] % DEPTH, DEPTH)

    def at_slot(self, slot):
        return (self.grp, self.base + 2 * self.z_of(slot))


def answer(slot):
    return SLOT[-NEAR[slot] % DEPTH]


def remote(source, target, send_sem, recv_sem, peer):
    return pltpu.make_async_remote_copy(
        src_ref=source, dst_ref=target, send_sem=send_sem, recv_sem=recv_sem,
        device_id=peer, device_id_type=MESH,
    )


def await_bytes(ref, sem):
    pltpu.make_async_copy(ref, ref, sem).wait()


def kernel(
    total_rows,
    features_hbm, means_hbm, variances_hbm, logits_ref,
    fresh_means_ref, fresh_variances_ref, fresh_weights_ref, rows_ref,
    features, means, variances, tiles, arrived, table, weights, log_weights, inputs,
    exponents, peaks, totals, shares, tally,
    core_out, core_in, own, plane_in, z_out, z_in, back, spread,
    counts_z, counts_plane, counts_pair,
    load_sems, z_send, z_recv, plane_send, plane_recv, pair_send, pair_recv,
    rz_send, rz_recv, rplane_send, rplane_recv, rpair_send, rpair_recv,
    bz_send, bz_recv, bplane_send, bplane_recv, bpair_send, bpair_recv,
    count_send, count_recv,
):
    me = Place()
    local_rows = features.shape[0]
    barrier = pltpu.get_barrier_semaphore()
    greeted = [me.at_slot(slot) for slot in range(DEPTH - 1, 0, -1)]
    greeted += [peer for peer, _ in me.plane] + [me.sibling]
    for peer in greeted:
        pl.semaphore_signal(barrier, inc=1, device_id=peer, device_id_type=MESH)
    loads = [
        pltpu.make_async_copy(source, target, load_sems.at[index])
        for index, (source, target) in enumerate(
            ((means_hbm, means), (variances_hbm, variances), (features_hbm, features))
        )
    ]
    for load in loads:
        load.start()
    loads[0].wait()
    loads[1].wait()
    for index in range(8):
        source = means if index < 4 else variances
        column, row = (index // 2) % 2, index % 2
        tiles[index] = source[row * 8 : row * 8 + 8, column * 128 : column * 128 + 128]
    arrived[0] = tiles[me.grp]
    pl.semaphore_wait(barrier, len(greeted))

    def send_along_z(source, target, send_sem, recv_sem_of):
        for slot in range(DEPTH - 1, 0, -1):
            there = answer(slot)
            remote(
                source, target.at[there], send_sem, recv_sem_of(there), me.at_slot(slot)
            ).start()

    def pass_on(buffer, target, z_sems, send_sems, recv_sems, meanwhile=None):
        for hop, (first, count) in enumerate(HOPS):
            held = buffer.at[pl.ds(first, count)]
            if hop > 0:
                await_bytes(held, z_sems.at[hop])
            for k in range(count):
                target[me.core, me.chip, first + k] = buffer[first + k]
            for peer, _ in me.plane:
                remote(
                    held, target.at[me.core, me.chip, pl.ds(first, count)],
                    send_sems.at[hop], recv_sems.at[hop], peer,
                ).start()
            if hop == 0 and meanwhile is not None:
                meanwhile()

    def hops_of(index):
        return [hop for hop, (first, _) in enumerate(HOPS) if first // 4 == index]

    def await_hop(target, hop, sems):
        first, count = HOPS[hop]
        await_bytes(target.at[0, pl.ds(0, PEERS), pl.ds(first, count)], sems.at[hop])

    def across(target, index, send_sems, recv_sems):
        part = target.at[me.core, pl.ds(0, 16), pl.ds(4 * index, 4)]
        return remote(part, part, send_sems.at[index], recv_sems.at[index], me.sibling)

    send_along_z(arrived.at[0], arrived, z_send.at[0], lambda slot: z_recv.at[HOP_OF[slot]])

    def prepare(step, carry):
        at = pl.multiple_of(step * 128, 128)
        x = features[pl.ds(at, 128), :]
        values = x.astype(F32)
        squared = values * values
        high = squared.astype(BF16)
        low = (squared - high.astype(F32)).astype(BF16)
        for index, value in enumerate((high, low, high, x, x)):
            inputs[pl.ds(at, 128), index * WIDTH : index * WIDTH + WIDTH] = value
        return carry

    def prepare_all():
        logits = logits_ref[...]
        top = jnp.max(logits)
        normal = logits - top - jnp.log(jnp.sum(jnp.exp(logits - top)))
        for piece in range(8):
            wide = jnp.broadcast_to(normal[piece : piece + 1, :], (128, 128))
            log_weights[piece * 128 : piece * 128 + 128, :] = jnp.transpose(wide)
        loads[2].wait()
        lax.fori_loop(0, local_rows // 128, prepare, 0)

    pass_on(arrived, table, z_recv, plane_send, plane_recv, prepare_all)

    def natural(slot, half):
        return pl.multiple_of(512 * half + 32 * me.z_of(slot), 32)

    def make_weights(index):
        for v in range(2):
            for k in range(4):
                slot = 4 * index + k
                here = pl.ds(natural(slot, v), 32)
                penalties = []
                for h in range(2):
                    def load(kind, column):
                        chips = [2 * (4 * kind + 2 * column + r) + v for r in range(2)]
                        return jnp.concatenate([table[h, chip, slot] for chip in chips], axis=0)

                    row = 128 * v + 32 * k + 16 * h
                    rows = slice(row, row + 16)
                    penalty = None
                    for column in range(2):
                        mean, variance = load(0, column), load(1, column)
                        inverse = 1.0 / variance
                        square_part = -0.5 * inverse
                        linear_part = mean * inverse
                        term = jnp.log(variance) + mean * linear_part
                        penalty = term if penalty is None else penalty + term
                        square_high = square_part.astype(BF16)
                        square_low = (square_part - square_high.astype(F32)).astype(BF16)
                        linear_high = linear_part.astype(BF16)
                        linear_low = (linear_part - linear_high.astype(F32)).astype(BF16)
                        for at, value in enumerate(
                            (square_high, square_high, square_low, linear_high, linear_low)
                        ):
                            at = at * WIDTH + column * 128
                            weights[index, rows, at : at + 128] = value
                    penalties.append(jnp.sum(penalty, axis=1, keepdims=True))
                log_weights[here, :] = (
                    log_weights[here, :]
                    - 0.5 * jnp.concatenate(penalties, axis=0)
                    - 0.5 * WIDTH * math.log(2.0 * math.pi)
                )

    def make_scores(index):
        offset = jnp.concatenate(
            [log_weights[pl.ds(natural(4 * index + k, v), 32), :] for v in range(2) for k in range(4)],
            axis=0,
        )
        offset = jnp.concatenate([offset] * (BLOCK // 128), axis=1)

        def visit(step, carry):
            at = pl.multiple_of(step * BLOCK, BLOCK)
            raw = lax.dot_general(
                weights[index], inputs[pl.ds(at, BLOCK), :], (((1,), (1,)), ((), ())),
                preferred_element_type=F32,
            )
            raw = raw + offset
            best = jnp.max(raw, axis=0, keepdims=True)
            value = jnp.exp(raw - best)
            exponents[index, :, pl.ds(at, BLOCK)] = value
            peaks[index : index + 1, pl.ds(at, BLOCK)] = best
            totals[index : index + 1, pl.ds(at, BLOCK)] = jnp.sum(value, axis=0, keepdims=True)
            return carry

        lax.fori_loop(0, local_rows // BLOCK, visit, 0, unroll=True)

    for index in range(GROUPS):
        for hop in hops_of(index):
            await_hop(table, hop, plane_recv)
        copy = across(table, index, pair_send, pair_recv)
        copy.start()
        copy.wait_recv()
        make_weights(index)
        make_scores(index)

    best = jnp.max(peaks[0:GROUPS, :], axis=0, keepdims=True)
    factors = jnp.exp(peaks[0:GROUPS, :] - best)
    total = jnp.sum(totals[0:GROUPS, :] * factors, axis=0, keepdims=True)
    row_scores = (best + jnp.log(total)) / WIDTH
    for piece in range(local_rows // 128):
        rows_ref[piece : piece + 1, :] = row_scores[:, piece * 128 : piece * 128 + 128]
    totals[0:GROUPS, :] = factors / total

    def rpair_copy(index):
        return remote(
            core_out.at[index], core_in.at[index], rpair_send.at[index], rpair_recv.at[index],
            me.sibling,
        )

    def share(index):
        sums = None
        for step in range(local_rows // BLOCK):
            at = step * BLOCK
            rounded = (
                exponents[index, :, at : at + BLOCK] * totals[index : index + 1, at : at + BLOCK]
            ).astype(BF16)
            shares[index, :, at : at + BLOCK] = rounded
            wide = rounded.astype(F32)
            wide = wide[:, :128] + wide[:, 128:]
            sums = wide if sums is None else sums + wide
        for v in range(2):
            for k in range(4):
                row = 128 * v + 32 * k
                tally[pl.ds(natural(4 * index + k, v), 32), :] = sums[row : row + 32]

    def moments(index, half, target):
        result = jnp.dot(
            shares[index, pl.ds(pl.multiple_of(128 * half, 128), 128), :],
            inputs[:, 2 * WIDTH : 4 * WIDTH],
            preferred_element_type=F32,
        )
        for k in range(4):
            for chip in range(16):
                row, column = 32 * k + 8 * (chip // 4), 128 * (chip % 4)
                target[index, chip, k] = result[row : row + 8, column : column + 128]

    def to_plane(index):
        rpair_copy(index).wait_recv()
        own[index] = own[index] + core_in[index]
        for offset, (peer, chip) in enumerate(me.plane):
            remote(
                own.at[index, chip], plane_in.at[index, offset],
                rplane_send.at[index], rplane_recv.at[index], peer,
            ).start()

    for index in range(GROUPS - 1, -1, -1):
        share(index)
        moments(index, 1 - me.core, core_out)
        rpair_copy(index).start()
        if index < GROUPS - 1:
            to_plane(index + 1)
        moments(index, me.core, own)
    to_plane(0)

    for piece in range(8):
        line = jnp.sum(jnp.transpose(tally[piece * 128 : piece * 128 + 128, :]), axis=0, keepdims=True)
        counts_pair[0, piece : piece + 1, :] = line
    for slot in range(DEPTH - 1, 0, -1):
        remote(
            counts_pair.at[0], counts_z.at[me.z], count_send.at[0], count_recv.at[0],
            me.at_slot(slot),
        ).start()
    counts_z[me.z] = counts_pair[0]

    for index in range(GROUPS - 1, -1, -1):
        await_bytes(plane_in.at[index], rplane_recv.at[index])
        reduced = own[index, me.chip]
        for offset in range(PEERS):
            reduced = reduced + plane_in[index, offset]
        z_out[pl.ds(4 * index, 4)] = reduced
        for slot in range(4 * index + 3, max(4 * index, 1) - 1, -1):
            remote(
                z_out.at[slot], z_in.at[answer(slot)], rz_send.at[0], rz_recv.at[0],
                me.at_slot(slot),
            ).start()

    await_bytes(counts_z.at[pl.ds(0, DEPTH - 1)], count_recv.at[0])
    counted = counts_z[0]
    for index in range(1, DEPTH):
        counted = counted + counts_z[index]
    counts_plane[me.chip] = counted
    for peer, _ in me.plane:
        remote(
            counts_plane.at[me.chip], counts_plane.at[me.chip], count_send.at[1], count_recv.at[1],
            peer,
        ).start()

    await_bytes(z_in.at[pl.ds(1, DEPTH - 1)], rz_recv.at[0])
    final = z_out[0]
    for slot in range(1, DEPTH):
        final = final + z_in[slot]
    back[0] = final
    send_along_z(back.at[0], back, bz_send.at[0], lambda slot: bz_recv.at[HOP_OF[slot]])

    await_bytes(counts_plane.at[pl.ds(0, PEERS)], count_recv.at[1])
    counted = counts_plane[0]
    for index in range(1, 16):
        counted = counted + counts_plane[index]
    counts_pair[1] = counted
    pair = remote(
        counts_pair.at[1], counts_pair.at[2], count_send.at[2], count_recv.at[2], me.sibling
    )
    pair.start()

    pass_on(back, spread, bz_recv, bplane_send, bplane_recv)

    pair.wait()
    denominator = counts_pair[1] + counts_pair[2] + 1.0
    fresh_weights_ref[...] = jnp.log(denominator / total_rows)
    inverse = 1.0 / denominator
    for piece in range(8):
        wide = jnp.broadcast_to(inverse[piece : piece + 1, :], (128, 128))
        tally[piece * 128 : piece * 128 + 128, :] = jnp.transpose(wide)

    await_bytes(z_in.at[pl.ds(1, DEPTH - 1)], z_send.at[0])
    await_bytes(z_in.at[pl.ds(1, DEPTH - 1)], count_send.at[0])
    await_bytes(z_in.at[pl.ds(1, DEPTH - 1)], count_send.at[1])
    await_bytes(z_in.at[pl.ds(1, DEPTH - 1)], rz_send.at[0])
    await_bytes(z_in.at[pl.ds(1, DEPTH - 1)], bz_send.at[0])
    for hop in range(len(HOPS)):
        await_hop(table, hop, plane_send)
    for index in range(GROUPS):
        await_bytes(plane_in.at[index], rplane_send.at[index])
        across(table, index, pair_send, pair_recv).wait_send()
        rpair_copy(index).wait_send()

    def update(index):
        across(spread, index, bpair_send, bpair_recv).wait_recv()
        for h in range(2):
            for k in range(4):
                slot = 4 * index + k
                first = natural(slot, h)
                for r in range(4):
                    here = pl.ds(pl.multiple_of(first + 8 * r, 8), 8)
                    scale = tally[here, :]
                    for c in range(2):
                        squares, linears = spread[h, 4 * r + c, slot], spread[h, 4 * r + 2 + c, slot]
                        mean = linears * scale
                        fresh_means_ref[here, c * 128 : c * 128 + 128] = mean
                        fresh_variances_ref[here, c * 128 : c * 128 + 128] = (
                            (squares + 1.0) * scale - mean * mean + 0.01
                        )

    for index in range(GROUPS):
        for hop in hops_of(index):
            await_hop(spread, hop, bplane_recv)
        across(spread, index, bpair_send, bpair_recv).start()
        if index > 0:
            update(index - 1)
    update(GROUPS - 1)
    for hop in range(len(HOPS)):
        await_hop(spread, hop, bplane_send)
    for index in range(GROUPS):
        across(spread, index, bpair_send, bpair_recv).wait_send()


def iterate(features, means, variances, logits, total_rows):
    rows = features.shape[0]
    dma = pltpu.SemaphoreType.DMA
    hbm = pl.BlockSpec(memory_space=pl.ANY)
    vmem = pl.BlockSpec(memory_space=pltpu.VMEM)
    tile = (8, 128)
    hops = len(HOPS)
    return pl.pallas_call(
        functools.partial(kernel, total_rows),
        out_shape=(
            jax.ShapeDtypeStruct((COMPS, WIDTH), F32),
            jax.ShapeDtypeStruct((COMPS, WIDTH), F32),
            jax.ShapeDtypeStruct(tile, F32),
            jax.ShapeDtypeStruct((rows // 128, 128), F32),
        ),
        in_specs=[hbm, hbm, hbm, vmem],
        out_specs=(vmem,) * 4,
        scratch_shapes=[
            pltpu.VMEM((rows, WIDTH), BF16),
            pltpu.VMEM((16, WIDTH), F32),
            pltpu.VMEM((16, WIDTH), F32),
            pltpu.VMEM((8, *tile), F32),
            pltpu.VMEM((DEPTH, *tile), F32),
            pltpu.VMEM((2, 16, DEPTH, *tile), F32),
            pltpu.VMEM((GROUPS, 256, 5 * WIDTH), BF16),
            pltpu.VMEM((COMPS, 128), F32),
            pltpu.VMEM((rows, 5 * WIDTH), BF16),
            pltpu.VMEM((GROUPS, 256, rows), F32),
            pltpu.VMEM((8, rows), F32),
            pltpu.VMEM((8, rows), F32),
            pltpu.VMEM((GROUPS, 256, rows), BF16),
            pltpu.VMEM((COMPS, 128), F32),
            pltpu.VMEM((GROUPS, 16, 4, *tile), F32),
            pltpu.VMEM((GROUPS, 16, 4, *tile), F32),
            pltpu.VMEM((GROUPS, 16, 4, *tile), F32),
            pltpu.VMEM((GROUPS, PEERS, 4, *tile), F32),
            pltpu.VMEM((DEPTH, *tile), F32),
            pltpu.VMEM((DEPTH, *tile), F32),
            pltpu.VMEM((DEPTH, *tile), F32),
            pltpu.VMEM((2, 16, DEPTH, *tile), F32),
            pltpu.VMEM((DEPTH, *tile), F32),
            pltpu.VMEM((16, *tile), F32),
            pltpu.VMEM((3, *tile), F32),
            dma((3,)),
            dma((1,)), dma((hops,)), dma((hops,)), dma((hops,)), dma((GROUPS,)), dma((GROUPS,)),
            dma((1,)), dma((1,)), dma((GROUPS,)), dma((GROUPS,)), dma((GROUPS,)), dma((GROUPS,)),
            dma((1,)), dma((hops,)), dma((hops,)), dma((hops,)), dma((GROUPS,)), dma((GROUPS,)),
            dma((3,)), dma((3,)),
        ],
        compiler_params=pltpu.CompilerParams(
            collective_id=0, has_side_effects=True, vmem_limit_bytes=56 << 20
        ),
    )(features, means, variances, logits)


def on_device(features, means, variances, weight_logits):
    rows = features.shape[0]
    total_rows = float(rows * lax.axis_size("grp") * lax.axis_size("comp") + COMPS)
    fresh_means, fresh_variances, fresh_weights, row_scores = iterate(
        features, means, variances, weight_logits.reshape(8, 128), total_rows
    )
    return fresh_means, fresh_variances, fresh_weights.reshape(COMPS), row_scores.reshape(rows)


def solution(mesh):
    return jax.shard_map(
        on_device,
        mesh=mesh,
        in_specs=(P(("grp", "comp"), None), P("comp", None), P("comp", None), P()),
        out_specs=(P(), P(), P(), P(("grp", "comp"))),
        check_vma=False,
    )
```

time: 106 us -> 88.8 us (0.84)
  Pallas kernels: 99 us -> 83.2 us
  other arithmetic: 5.13 us -> 0 us
  local copies, waits for them, and re-layouts: 0.6 us -> 4.63 us
    pallas_call x1, Pallas kernels: 99 us -> 83.2 us  [iterate(): pl.pallas_call(functools.partial(kernel, total_rows), out_shape=(jax.Shap...]
    unnamed x3 -> x10, local copies, waits for them, and re-layouts: 0.6 us -> 4.63 us
    add x2 -> x0, other arithmetic: 3.85 us -> none  [the longest x1 3.16 us: update_step(): (squares + 1.0) / denominator - fresh_means * fresh_means + 0.01]
    log x1 -> x0, other arithmetic: 1.28 us -> none  [update_step(): fresh_weights = jnp.log((counts + 1.0) / total_rows)]
where the time goes in v3:
time: 88.8 us; the launch traced here: 88.5 us
  Pallas kernels  83.2 us (94%)
  local copies, waits for them, and re-layouts  4.63 us (5%)
    pallas_call x1, Pallas kernels, iterate(): pl.pallas_call(functools.partial(kernel, total_rows), out_shape=(jax.Shap...  83.2 us
    unnamed x10, local copies, waits for them, and re-layouts  4.63 us

profile of v3, /device:TPU:1, one launch (start us, length us, event | category | flops | bytes accessed | tf_op | source)
XLA Modules:
  0.0 88.5 jit_solution(4639678660816867760)
XLA Ops:
  0.6 83.2 %shard_map.75 = (f32[1024,256]{1,0:T(8,128)}, f32[1024,256]{1,0:T(8,128)}, f32[8,128]{1,0:T(8,128)}, f32[16,128]{1,0:T(8,128)}) custom-call(bf16[2048,256]{1,0:T(8,128)(2,1)} %features_hbm.1, f32[16,256]{1,0:T(8,128)} %means_hbm.1, f32[16,256]{1,0:T(8,128)} %variances_hbm.1, f32[8,128]{1,0:T(8,128)} %bitcast.4), custom_call_target="tpu_custom_call" | custom-call | tf_op jit(solution)/shard_map/pallas_call | solution.py:405
  83.8 0.0 copy-start
  83.9 2.4 %copy.12 = f32[1024,256]{1,0:T(8,128)} copy(f32[1024,256]{1,0:T(8,128)} %get-tuple-element.16) | data formatting | bytes 2097152
  86.2 0.0 copy-done
  86.2 0.0 copy-start.2
  86.2 1.0 %copy.13 = f32[1024,256]{1,0:T(8,128)} copy(f32[1024,256]{1,0:T(8,128)S(1)} %copy-done) | data formatting | bytes 2097152
  87.2 0.0 copy-done.2
  87.2 0.0 copy-start.1
  87.2 0.6 copy.14
  87.8 0.1 copy-done.1
  87.9 0.6 copy.15
Async XLA Ops:
  83.8 2.4 %copy-start = (f32[1024,256]{1,0:T(8,128)S(1)}, f32[1024,256]{1,0:T(8,128)}, u32[]{:S(2)}) copy-start(f32[1024,256]{1,0:T(8,128)} %get-tuple-element.17) | copy-start | bytes 3145732
  86.2 1.0 %copy-start.2 = (f32[8,128]{1,0:T(8,128)S(1)}, f32[8,128]{1,0:T(8,128)}, u32[]{:S(2)}) copy-start(f32[8,128]{1,0:T(8,128)} %get-tuple-element.10) | copy-start | bytes 12292
  87.2 0.7 copy-start.1

commit v4 on v3

--- a/solution.py
+++ b/solution.py
@@ -16,7 +16,7 @@
 DEPTH = 16
 OFFSETS = sorted(
     ((dx, dy) for dx in range(4) for dy in range(4) if (dx, dy) != (0, 0)),
-    key=lambda d: (min(d[0], 4 - d[0]) + min(d[1], 4 - d[1]), d),
+    key=lambda d: (-min(d[0], 4 - d[0]) - min(d[1], 4 - d[1]), d),
 )
 PEERS = len(OFFSETS)
 NEAR = (0, 1, -1, 2, -2, 3, -3, 4, -4, 5, -5, 6, -6, 7, -7, 8)
@@ -450,11 +450,45 @@
     )(features, means, variances, logits)
 
 
+def hand_on_kernel(*refs):
+    sources, targets, holds, sems = refs[:4], refs[4:8], refs[8:12], refs[12]
+    loads, stores = [], []
+    for source, target, hold in zip(sources, targets, holds):
+        pieces = 4 if source.shape[0] == COMPS else 1
+        size = source.shape[0] // pieces
+        for piece in range(pieces):
+            part = pl.ds(piece * size, size)
+            at = len(loads)
+            loads.append(pltpu.make_async_copy(source.at[part], hold.at[part], sems.at[0, at]))
+            stores.append(pltpu.make_async_copy(hold.at[part], target.at[part], sems.at[1, at]))
+    for load in loads:
+        load.start()
+    for load, store in zip(loads, stores):
+        load.wait()
+        store.start()
+    for store in stores:
+        store.wait()
+
+
+def hand_on(*arrays):
+    anywhere = pl.BlockSpec(memory_space=pl.ANY)
+    return pl.pallas_call(
+        hand_on_kernel,
+        out_shape=tuple(jax.ShapeDtypeStruct(a.shape, a.dtype) for a in arrays),
+        in_specs=[anywhere] * 4,
+        out_specs=(anywhere,) * 4,
+        scratch_shapes=[
+            *(pltpu.VMEM(a.shape, a.dtype) for a in arrays),
+            pltpu.SemaphoreType.DMA((2, 10)),
+        ],
+    )(*arrays)
+
+
 def on_device(features, means, variances, weight_logits):
     rows = features.shape[0]
     total_rows = float(rows * lax.axis_size("grp") * lax.axis_size("comp") + COMPS)
-    fresh_means, fresh_variances, fresh_weights, row_scores = iterate(
-        features, means, variances, weight_logits.reshape(8, 128), total_rows
+    fresh_means, fresh_variances, fresh_weights, row_scores = hand_on(
+        *iterate(features, means, variances, weight_logits.reshape(8, 128), total_rows)
     )
     return fresh_means, fresh_variances, fresh_weights.reshape(COMPS), row_scores.reshape(rows)
 

time: 88.8 us -> 83.7 us (0.943)
  local copies, waits for them, and re-layouts: 4.63 us -> 0 us
    unnamed x10 -> x0, local copies, waits for them, and re-layouts: 4.63 us -> none
    pallas_call x1, Pallas kernels: 83.2 us -> 80.4 us  [iterate(): pl.pallas_call(functools.partial(kernel, total_rows), out_shape=(jax.Shap...]
    pallas_call x0 -> x1, Pallas kernels: none -> 2.44 us  [hand_on(): pl.pallas_call(hand_on_kernel, out_shape=tuple((jax.ShapeDtypeStruct(a.sh...]
where the time goes in v4:
time: 83.7 us; the launch traced here: 83.5 us
  Pallas kernels  82.9 us (99%)
    pallas_call x1, Pallas kernels, iterate(): pl.pallas_call(functools.partial(kernel, total_rows), out_shape=(jax.Shap...  80.4 us
    pallas_call x1, Pallas kernels, hand_on(): pl.pallas_call(hand_on_kernel, out_shape=tuple((jax.ShapeDtypeStruct(a.sh...  2.44 us

profile of v4, /device:TPU:1, one launch (start us, length us, event | category | flops | bytes accessed | tf_op | source)
XLA Modules:
  0.0 83.5 jit_solution(1559736422769000945)
XLA Ops:
  0.6 80.4 %shard_map.75 = (f32[1024,256]{1,0:T(8,128)}, f32[1024,256]{1,0:T(8,128)}, f32[8,128]{1,0:T(8,128)}, f32[16,128]{1,0:T(8,128)}) custom-call(bf16[2048,256]{1,0:T(8,128)(2,1)} %features_hbm.1, f32[16,256]{1,0:T(8,128)} %means_hbm.1, f32[16,256]{1,0:T(8,128)} %variances_hbm.1, f32[8,128]{1,0:T(8,128)} %bitcast.3), custom_call_target="tpu_custom_call" | custom-call | tf_op jit(solution)/shard_map/pallas_call | solution.py:405
  81.1 2.4 %shard_map.76 = (f32[1024,256]{1,0:T(8,128)}, f32[1024,256]{1,0:T(8,128)}, f32[8,128]{1,0:T(8,128)}, f32[16,128]{1,0:T(8,128)}) custom-call(f32[1024,256]{1,0:T(8,128)} %get-tuple-element.12.refs_0_, f32[1024,256]{1,0:T(8,128)} %get-tuple-element.13.refs_1_, f32[8,128]{1,0:T(8,128)} %get-tuple-element.14.refs_2_, f32[16,128]{1,0:T(8,128)} %get-tuple-element.15.refs_3_), custom_call_target="tpu_custom_call" | custom-call | tf_op jit(solution)/shard_map/pallas_call | solution.py:475

commit v5 on v4

--- a/solution.py
+++ b/solution.py
@@ -73,7 +73,7 @@
     fresh_means_ref, fresh_variances_ref, fresh_weights_ref, rows_ref,
     features, means, variances, tiles, arrived, table, weights, log_weights, inputs,
     exponents, peaks, totals, shares, tally,
-    core_out, core_in, own, plane_in, z_out, z_in, back, spread,
+    both, core_in, plane_in, z_out, z_in, back, spread,
     counts_z, counts_plane, counts_pair,
     load_sems, z_send, z_recv, plane_send, plane_recv, pair_send, pair_recv,
     rz_send, rz_recv, rplane_send, rplane_recv, rpair_send, rpair_recv,
@@ -225,26 +225,29 @@
 
         lax.fori_loop(0, local_rows // BLOCK, visit, 0, unroll=True)
 
-    for index in range(GROUPS):
+    def pair_up(index):
         for hop in hops_of(index):
             await_hop(table, hop, plane_recv)
-        copy = across(table, index, pair_send, pair_recv)
-        copy.start()
-        copy.wait_recv()
+        across(table, index, pair_send, pair_recv).start()
+
+    pair_up(0)
+    for index in range(GROUPS):
+        across(table, index, pair_send, pair_recv).wait_recv()
         make_weights(index)
+        if index + 1 < GROUPS:
+            pair_up(index + 1)
         make_scores(index)
 
     best = jnp.max(peaks[0:GROUPS, :], axis=0, keepdims=True)
     factors = jnp.exp(peaks[0:GROUPS, :] - best)
     total = jnp.sum(totals[0:GROUPS, :] * factors, axis=0, keepdims=True)
-    row_scores = (best + jnp.log(total)) / WIDTH
-    for piece in range(local_rows // 128):
-        rows_ref[piece : piece + 1, :] = row_scores[:, piece * 128 : piece * 128 + 128]
+    peaks[7:8, :] = best
+    totals[7:8, :] = total
     totals[0:GROUPS, :] = factors / total
 
     def rpair_copy(index):
         return remote(
-            core_out.at[index], core_in.at[index], rpair_send.at[index], rpair_recv.at[index],
+            both.at[index, 1 - me.core], core_in.at[index], rpair_send.at[index], rpair_recv.at[index],
             me.sibling,
         )
 
@@ -264,34 +267,36 @@
                 row = 128 * v + 32 * k
                 tally[pl.ds(natural(4 * index + k, v), 32), :] = sums[row : row + 32]
 
-    def moments(index, half, target):
+    def moments(index):
         result = jnp.dot(
-            shares[index, pl.ds(pl.multiple_of(128 * half, 128), 128), :],
-            inputs[:, 2 * WIDTH : 4 * WIDTH],
-            preferred_element_type=F32,
+            shares[index], inputs[:, 2 * WIDTH : 4 * WIDTH], preferred_element_type=F32
         )
-        for k in range(4):
-            for chip in range(16):
-                row, column = 32 * k + 8 * (chip // 4), 128 * (chip % 4)
-                target[index, chip, k] = result[row : row + 8, column : column + 128]
+        for v in range(2):
+            for k in range(4):
+                for chip in range(16):
+                    row, column = 128 * v + 32 * k + 8 * (chip // 4), 128 * (chip % 4)
+                    both[index, v, chip, k] = result[row : row + 8, column : column + 128]
 
     def to_plane(index):
         rpair_copy(index).wait_recv()
-        own[index] = own[index] + core_in[index]
+        both[index, me.core] = both[index, me.core] + core_in[index]
         for offset, (peer, chip) in enumerate(me.plane):
             remote(
-                own.at[index, chip], plane_in.at[index, offset],
+                both.at[index, me.core, chip], plane_in.at[index, offset],
                 rplane_send.at[index], rplane_recv.at[index], peer,
             ).start()
 
     for index in range(GROUPS - 1, -1, -1):
         share(index)
-        moments(index, 1 - me.core, core_out)
+        moments(index)
         rpair_copy(index).start()
         if index < GROUPS - 1:
             to_plane(index + 1)
-        moments(index, me.core, own)
     to_plane(0)
+
+    row_scores = (peaks[7:8, :] + jnp.log(totals[7:8, :])) / WIDTH
+    for piece in range(local_rows // 128):
+        rows_ref[piece : piece + 1, :] = row_scores[:, piece * 128 : piece * 128 + 128]
 
     for piece in range(8):
         line = jnp.sum(jnp.transpose(tally[piece * 128 : piece * 128 + 128, :]), axis=0, keepdims=True)
@@ -305,7 +310,7 @@
 
     for index in range(GROUPS - 1, -1, -1):
         await_bytes(plane_in.at[index], rplane_recv.at[index])
-        reduced = own[index, me.chip]
+        reduced = both[index, me.core, me.chip]
         for offset in range(PEERS):
             reduced = reduced + plane_in[index, offset]
         z_out[pl.ds(4 * index, 4)] = reduced
@@ -427,8 +432,7 @@
             pltpu.VMEM((8, rows), F32),
             pltpu.VMEM((GROUPS, 256, rows), BF16),
             pltpu.VMEM((COMPS, 128), F32),
-            pltpu.VMEM((GROUPS, 16, 4, *tile), F32),
-            pltpu.VMEM((GROUPS, 16, 4, *tile), F32),
+            pltpu.VMEM((GROUPS, 2, 16, 4, *tile), F32),
             pltpu.VMEM((GROUPS, 16, 4, *tile), F32),
             pltpu.VMEM((GROUPS, PEERS, 4, *tile), F32),
             pltpu.VMEM((DEPTH, *tile), F32),

time: 83.7 us -> 82.6 us (0.987)
  Pallas kernels: 82.9 us -> 81.7 us
    pallas_call x1, Pallas kernels: 80.4 us -> 79.3 us  [iterate(): pl.pallas_call(functools.partial(kernel, total_rows), out_shape=(jax.Shap...]
where the time goes in v5:
time: 82.6 us; the launch traced here: 82.3 us
  Pallas kernels  81.7 us (99%)
    pallas_call x1, Pallas kernels, iterate(): pl.pallas_call(functools.partial(kernel, total_rows), out_shape=(jax.Shap...  79.3 us
    pallas_call x1, Pallas kernels, hand_on(): pl.pallas_call(hand_on_kernel, out_shape=tuple((jax.ShapeDtypeStruct(a.sh...  2.44 us

profile of v5, /device:TPU:1, one launch (start us, length us, event | category | flops | bytes accessed | tf_op | source)
XLA Modules:
  0.0 82.3 jit_solution(12136002095436553974)
XLA Ops:
  0.6 79.3 %shard_map.75 = (f32[1024,256]{1,0:T(8,128)}, f32[1024,256]{1,0:T(8,128)}, f32[8,128]{1,0:T(8,128)}, f32[16,128]{1,0:T(8,128)}) custom-call(bf16[2048,256]{1,0:T(8,128)(2,1)} %features_hbm.1, f32[16,256]{1,0:T(8,128)} %means_hbm.1, f32[16,256]{1,0:T(8,128)} %variances_hbm.1, f32[8,128]{1,0:T(8,128)} %bitcast.3), custom_call_target="tpu_custom_call" | custom-call | tf_op jit(solution)/shard_map/pallas_call | solution.py:410
  79.9 2.4 %shard_map.76 = (f32[1024,256]{1,0:T(8,128)}, f32[1024,256]{1,0:T(8,128)}, f32[8,128]{1,0:T(8,128)}, f32[16,128]{1,0:T(8,128)}) custom-call(f32[1024,256]{1,0:T(8,128)} %get-tuple-element.12.refs_0_, f32[1024,256]{1,0:T(8,128)} %get-tuple-element.13.refs_1_, f32[8,128]{1,0:T(8,128)} %get-tuple-element.14.refs_2_, f32[16,128]{1,0:T(8,128)} %get-tuple-element.15.refs_3_), custom_call_target="tpu_custom_call" | custom-call | tf_op jit(solution)/shard_map/pallas_call | solution.py:479
